TPU v7x, 32 devices: a whole 2x2x4 slice. The times are simulated.
32 devices in a mesh: seq: 16 (over z, y, x), head: 2 (over core).
Axes of the slice: x: 2, y: 2, z: 4, core: 2. Of those that a mesh axis runs over, the one named last changes fastest.
Arguments:
- queries: bfloat16 [4096, 128], P('seq'), may hold values from -6 to 6
- keys: bfloat16 [4096, 128], P('seq'), may hold values from -6 to 6
- values: bfloat16 [4096, 2048], P('seq', 'head'), may hold values from -6 to 6
- out_grad: bfloat16 [4096, 2048], P('seq', 'head'), may hold values from -6 to 6
- raw_trans: float32 [16, 128, 128], P('seq'), may hold values from -1 to 1, as said below
Outputs:
- outputs: bfloat16 [4096, 2048], P('seq', 'head')
- grad_queries: bfloat16 [4096, 128], P(('seq', 'head'))
- grad_keys: bfloat16 [4096, 128], P(('seq', 'head'))
- grad_values: bfloat16 [4096, 2048], P('seq', 'head')
- grad_trans: float32 [128, 16, 128], P('head', 'seq')
Inputs may be any that keep to these rules, and one draw needn't show every extreme that they name: Every block of raw_trans has a positive diagonal.
All inputs are finite; a program needn't handle non-finite values.
Results may differ from a plain program's by a relative error of at most 0.019.
Values may be sent and summed in bfloat16 or wider, within the bound.
A program may use at most 64 MiB of HBM per device.

v0:
```python
import math

import jax
import jax.numpy as jnp
from jax import lax
from jax.sharding import PartitionSpec as P

STATE_ROWS = 128
P_SIZE = 256
L = 256


PRECISE = lax.Precision.HIGHEST


def prefix(part, axis, combine, identity, reverse):
    count = lax.axis_size(axis)
    place = lax.axis_index(axis)
    ahead = count - 1 - place if reverse else place
    gathered = jax.tree.map(lambda a: lax.all_gather(a, axis), part)
    state = jax.tree.map(lambda a, e: jnp.zeros_like(a) + jnp.asarray(e, a.dtype), part, identity)

    def one(lap, state):
        source = count - 1 - lap if reverse else lap
        return combine(
            state, jax.tree.map(lambda a: lax.dynamic_index_in_dim(a, source, 0, False), gathered)
        )

    return lax.fori_loop(0, ahead, one, state)


def normalize_blocks(raw):
    count = raw.shape[-1]
    vector = jnp.ones(raw.shape[:-1], jnp.float32) / math.sqrt(count)
    for repeat in range(6):
        product = jnp.einsum("cij,cj->ci", raw, vector, precision=PRECISE)
        returned = jnp.einsum("cji,cj->ci", raw, product, precision=PRECISE)
        vector = returned / jnp.sqrt(jnp.sum(returned * returned, axis=-1, keepdims=True))
    product = jnp.einsum("cij,cj->ci", raw, vector, precision=PRECISE)
    spectral = jnp.sqrt(jnp.sum(product * product, axis=-1))
    return raw / spectral[:, None, None]


def compose(earlier, later):
    matrix_early, vector_early = earlier
    matrix_late, vector_late = later
    return (
        jnp.dot(matrix_late, matrix_early, precision=PRECISE),
        jnp.dot(matrix_late, vector_early, precision=PRECISE) + vector_late,
    )


def fold_blocks(running, pieces):
    return (compose(running, pieces), None)


def per_device(queries, keys, values, out_grad, raw_trans):
    spans = raw_trans.shape[0]
    state_dim = raw_trans.shape[1]
    col_count = values.shape[1]
    heads_here = col_count // P_SIZE
    block_len = queries.shape[0] // spans
    attn_scale = 0.5 / math.sqrt(STATE_ROWS * L)
    transition = normalize_blocks(raw_trans)
    flipped = jnp.swapaxes(transition, 1, 2)
    query_blocks = queries.reshape(spans, block_len, state_dim)
    key_blocks = keys.reshape(spans, block_len, state_dim)
    value_blocks = values.reshape(spans, block_len, col_count)
    grad_blocks = out_grad.reshape(spans, block_len, col_count)
    causal = jnp.arange(block_len)[:, None] >= jnp.arange(block_len)[None, :]
    identity = jnp.eye(state_dim, dtype=jnp.float32)
    empty_state = jnp.zeros((state_dim, col_count), jnp.float32)
    updates = jnp.einsum(
        "cln,clp->cnp", key_blocks, value_blocks, preferred_element_type=jnp.float32
    )
    (agg_matrix, agg_state), unused = lax.scan(
        fold_blocks, (identity, empty_state), (transition, updates)
    )
    inflow = attn_scale * jnp.einsum(
        "cln,clp->cnp", query_blocks, grad_blocks, preferred_element_type=jnp.float32
    )
    (back_matrix, back_vector), unused_back = lax.scan(
        fold_blocks, (identity, empty_state), (flipped, inflow), reverse=True
    )
    prefix_matrix, enter_state = prefix(
        (agg_matrix, agg_state), "seq", compose, (identity, empty_state), False
    )
    suffix_matrix, enter_grad = prefix(
        (back_matrix, back_vector), "seq", compose, (identity, empty_state), True
    )

    def advance(state_now, pieces):
        matrix, update = pieces
        return (
            jnp.dot(matrix, state_now, precision=PRECISE) + update,
            state_now.astype(jnp.bfloat16),
        )

    last_state, state_lows = lax.scan(advance, enter_state, (transition, updates))
    scores = jnp.einsum(
        "cln,cmn->clm", query_blocks, key_blocks, preferred_element_type=jnp.float32
    )
    weights = jnp.where(causal, attn_scale * scores, 0.0).astype(jnp.bfloat16)
    outputs = attn_scale * jnp.einsum(
        "cln,cnp->clp", query_blocks, state_lows, preferred_element_type=jnp.float32
    ) + jnp.einsum("clm,cmp->clp", weights, value_blocks, preferred_element_type=jnp.float32)
    outputs = outputs.astype(jnp.bfloat16).reshape(spans * block_len, col_count)

    def retreat(carried, pieces):
        matrix_flip, inflow_now = pieces
        return (
            inflow_now + jnp.dot(matrix_flip, carried, precision=PRECISE),
            carried.astype(jnp.bfloat16),
        )

    first_grad, carried_lows = lax.scan(retreat, enter_grad, (flipped, inflow), reverse=True)
    grad_values = jnp.einsum(
        "cml,cmp->clp", weights, grad_blocks, preferred_element_type=jnp.float32
    ) + jnp.einsum("cln,cnp->clp", key_blocks, carried_lows, preferred_element_type=jnp.float32)
    grad_values = grad_values.astype(jnp.bfloat16).reshape(spans * block_len, col_count)
    heads_grad = grad_blocks.reshape(spans, block_len, heads_here, P_SIZE)
    heads_value = value_blocks.reshape(spans, block_len, heads_here, P_SIZE)
    dscore = jnp.einsum(
        "clhp,cmhp->chlm", heads_grad, heads_value, preferred_element_type=jnp.float32
    )
    score_grad = jnp.where(causal[None, None], attn_scale * dscore, 0.0).astype(jnp.bfloat16)
    query_part = attn_scale * jnp.einsum(
        "clp,cnp->cln", grad_blocks, state_lows, preferred_element_type=jnp.float32
    ) + jnp.einsum("chlm,cmn->cln", score_grad, key_blocks, preferred_element_type=jnp.float32)
    key_part = jnp.einsum(
        "clp,cnp->cln", value_blocks, carried_lows, preferred_element_type=jnp.float32
    ) + jnp.einsum("chlm,cln->cmn", score_grad, query_blocks, preferred_element_type=jnp.float32)
    query_part = query_part.reshape(spans * block_len, state_dim)
    key_part = key_part.reshape(spans * block_len, state_dim)
    row_share = state_dim // lax.axis_size("head")
    row_start = lax.axis_index("head") * row_share
    grad_piece = lax.all_gather(carried_lows, "head", axis=2, tiled=True)
    state_piece = lax.all_gather(state_lows, "head", axis=2, tiled=True)
    own_rows = lax.dynamic_slice_in_dim(grad_piece, row_start, row_share, 1)
    grad_trans = jnp.einsum(
        "cnp,cmp->ncm", own_rows, state_piece, preferred_element_type=jnp.float32
    )
    grad_queries, grad_keys = (
        lax.psum_scatter(
            query_part.astype(jnp.bfloat16), "head", scatter_dimension=0, tiled=True
        ).astype(jnp.float32),
        lax.psum_scatter(
            key_part.astype(jnp.bfloat16), "head", scatter_dimension=0, tiled=True
        ).astype(jnp.float32),
    )
    return (
        outputs,
        grad_queries.astype(jnp.bfloat16),
        grad_keys.astype(jnp.bfloat16),
        grad_values,
        grad_trans,
    )


def solution(mesh):
    in_specs = (
        P("seq", None),
        P("seq", None),
        P("seq", "head"),
        P("seq", "head"),
        P("seq", None, None),
    )
    out_specs = (
        P("seq", "head"),
        P(("seq", "head"), None),
        P(("seq", "head"), None),
        P("seq", "head"),
        P("head", "seq", None),
    )
    return jax.shard_map(
        per_device, mesh=mesh, in_specs=in_specs, out_specs=out_specs, check_vma=False
    )
```

profile of v0, /device:TPU:0, one launch (start us, length us, event | category | flops | bytes accessed | tf_op | source)
XLA Modules:
  0.0 430.7 jit_solution(12297222011920843000)
XLA Ops:
  7.2 1.0 convolution_bitcast_fusion.14
  8.2 1.7 multiply_reduce_fusion.5
  10.6 1.0 convolution_bitcast_fusion.12
  11.6 1.7 multiply_reduce_fusion.4
  14.0 1.0 convolution_bitcast_fusion.10
  15.0 1.7 multiply_reduce_fusion.3
  17.3 1.0 convolution_bitcast_fusion.8
  18.4 1.7 multiply_reduce_fusion.2
  20.7 1.0 convolution_bitcast_fusion.6
  21.7 1.7 multiply_reduce_fusion.1
  24.1 1.0 convolution_bitcast_fusion.4
  25.1 1.7 multiply_reduce_fusion
  27.5 1.7 fusion.22
  29.8 1.7 fusion.34
  31.6 1.3 fusion.29
  32.9 2.1 fusion.13
  35.1 1.6 fusion.37
  36.8 1.2 fusion.31
  38.0 2.1 convolution_add_fusion.4
  40.2 1.6 fusion.12
  43.1 46.6 %all-gather.15.cloned.1.call-done = f32[2048,128]{1,0:T(8,128)} async-done(((f32[128,128]{1,0:T(8,128)}), f32[2048,128]{1,0:T(8,128)}) %all-gather.15.cloned.1.call-update) | async-done | bytes 1048592 | tf_op jit(solution)/shard_map/all_gather | solution.py:20
  89.7 115.0 %all-gather.17.cloned.1.call-done = f32[2048,1024]{1,0:T(8,128)} async-done(((f32[128,1024]{1,0:T(8,128)}), f32[2048,1024]{1,0:T(8,128)}) %all-gather.17.cloned.1.call-update) | async-done | bytes 8388624 | tf_op jit(solution)/shard_map/all_gather | solution.py:20
  204.8 26.1 %while.17 = (s32[]{:T(128)}, f32[128,1024]{1,0:T(8,128)S(1)}, s32[]{:T(128)}, f32[16,128,128]{2,1,0:T(8,128)}, f32[16,128,1024]{2,1,0:T(8,128)}, /*index=5*/s32[]{:T(128)}, s32[]{:T(128)}, s32[]{:T(128)}, s32[]{:T(128)}) while((s32[]{:T(128)}, f32[128,1024]{1,0:T(8,128)S(1)}, s32[]{:T(128)}, f32[16,128,128]{2,1,0:T(8,128)}, ...), condition=%wide.region_12.13_spmd, body=%wide.region_11.12_spmd.sunk | while | flops 201457664 | bytes 2688139 | solution.py:29
  204.8 1.7 convolution_add_fusion.8
  206.6 1.7 convolution_add_fusion.8
  208.3 1.7 convolution_add_fusion.8
  210.1 1.7 convolution_add_fusion.8
  211.8 1.7 convolution_add_fusion.8
  213.6 1.7 convolution_add_fusion.8
  215.3 1.7 convolution_add_fusion.8
  217.0 1.7 convolution_add_fusion.8
  218.8 1.7 convolution_add_fusion.8
  220.5 1.7 convolution_add_fusion.8
  222.3 1.7 convolution_add_fusion.8
  224.0 1.7 convolution_add_fusion.8
  225.7 1.7 convolution_add_fusion.8
  227.5 1.7 convolution_add_fusion.8
  229.2 1.7 convolution_add_fusion.8
  230.9 2.3 all-gather.5
  233.6 27.4 %all-gather.11.cloned.1.call-done = f32[2048,128]{1,0:T(8,128)} async-done(((f32[128,128]{1,0:T(8,128)}), f32[2048,128]{1,0:T(8,128)}) %all-gather.11.cloned.1.call-update) | async-done | bytes 1048592 | tf_op jit(solution)/shard_map/all_gather | solution.py:20
  261.0 114.9 %all-gather.13.cloned.1.call-done = f32[2048,1024]{1,0:T(8,128)} async-done(((f32[128,1024]{1,0:T(8,128)}), f32[2048,1024]{1,0:T(8,128)}) %all-gather.13.cloned.1.call-update) | async-done | bytes 8388624 | tf_op jit(solution)/shard_map/all_gather | solution.py:20
  376.7 1.0 copy.26
  377.7 1.1 fusion.11
  378.8 1.2 fusion.20
  381.8 2.2 all-gather.4
  384.0 1.9 fusion.27
  385.9 26.7 %reduce-scatter.9.cloned.1.call-done = bf16[128,128]{1,0:T(8,128)(2,1)} async-done(((bf16[256,128]{1,0:T(8,128)(2,1)}), bf16[128,128]{1,0:T(8,128)(2,1)}) %reduce-scatter.9.cloned.1.call-update) | async-done | bytes 32784
  412.6 11.3 %reduce-scatter.7.cloned.1.call-done = bf16[128,128]{1,0:T(8,128)(2,1)} async-done(((bf16[256,128]{1,0:T(8,128)(2,1)}), bf16[128,128]{1,0:T(8,128)(2,1)}) %reduce-scatter.7.cloned.1.call-update) | async-done | bytes 32784
  (50 shorter events, 5.2 us)
Async XLA Ops:
  7.2 30.9 %copy-start = (bf16[256,128]{1,0:T(8,128)(2,1)S(1)}, bf16[256,128]{1,0:T(8,128)(2,1)}, u32[]{:S(2)}) copy-start(bf16[256,128]{1,0:T(8,128)(2,1)} %param.10) | copy-start | bytes 196612
  7.2 34.6 %copy-start.3 = (bf16[256,128]{1,0:T(8,128)(2,1)S(1)}, bf16[256,128]{1,0:T(8,128)(2,1)}, u32[]{:S(2)}) copy-start(bf16[256,128]{1,0:T(8,128)(2,1)} %param.9) | copy-start | bytes 196612
  7.2 82.5 %all-gather.15.cloned.1.call-start = ((), (), s32[]{:S(2)}) async-start(), calls=%async_computation.4 | async-start | bytes 1114112 | tf_op jit(solution)/shard_map/all_gather | solution.py:20
  31.6 173.2 %all-gather.17.cloned.1.call-start = ((), (), s32[]{:S(2)}) async-start(), calls=%async_computation.5 | async-start | bytes 8912896 | tf_op jit(solution)/shard_map/all_gather | solution.py:20
  35.0 225.9 %all-gather.11.cloned.1.call-start = ((), (), s32[]{:S(2)}) async-start(), calls=%async_computation.2 | async-start | bytes 1114112 | tf_op jit(solution)/shard_map/all_gather | solution.py:20
  36.8 339.1 %all-gather.13.cloned.1.call-start = ((), (), s32[]{:S(2)}) async-start(), calls=%async_computation.3 | async-start | bytes 8912896 | tf_op jit(solution)/shard_map/all_gather | solution.py:20
  40.1 372.5 %reduce-scatter.9.cloned.1.call-start = ((), (), s32[]{:S(2)}) async-start(), calls=%async_computation.7 | async-start | bytes 98304
  233.5 142.8 %copy-start.1 = (bf16[256,1024]{1,0:T(8,128)(2,1)S(1)}, bf16[256,1024]{1,0:T(8,128)(2,1)}, u32[]{:S(2)}) copy-start(bf16[256,1024]{1,0:T(8,128)(2,1)} %param.11) | copy-start | bytes 1572868
  375.9 1.8 copy-start.2
  380.7 43.1 %reduce-scatter.7.cloned.1.call-start = ((), (), s32[]{:S(2)}) async-start(), calls=%async_computation.6 | async-start | bytes 98304
Sparse Core Ops, SparseCore 0:
  31.7 57.9 all-gather.14
  93.1 111.6 all-gather.16
  207.5 53.4 all-gather.10
  264.2 111.6 all-gather.12
  380.9 31.6 reduce-scatter.8
  415.2 8.6 reduce-scatter.6
where the time goes:
time: 432 us; the launch traced here: 431 us
  waiting for transfers between devices  342 us (79%)
  matrix products  61 us (14%)
  between operations  19.1 us (4%)
  blocking collectives  4.48 us (1%)
    all_gather x4, waiting for transfers between devices, prefix(): gathered = jax.tree.map(lambda a: lax.all_gather(a, axis), part)  304 us
    unnamed x8, waiting for transfers between devices  38.1 us
    dot_general x17, matrix products, compose(): jnp.dot(matrix_late, vector_early, precision=PRECISE) + vector_late  27.4 us
    dot_general x6, matrix products, normalize_blocks(): returned = jnp.einsum('cji,cj->ci', raw, product, precision=PRECISE)  9.99 us
  transfers between devices with their start and end apart: 6, of which 6 were waited for; matrix products, arithmetic and copies ran while one was open for 9% of the time, Pallas kernels for 0%

commit v1 on v0

v1 whole, which is shorter than its diff:
```python
import functools
import math

import jax
import jax.numpy as jnp
from jax import lax
from jax.experimental import pallas as pl
from jax.experimental.pallas import tpu as pltpu
from jax.sharding import PartitionSpec as P

STATE_ROWS = 128
P_SIZE = 256
L = 256

F32 = jnp.float32
BF16 = jnp.bfloat16
MESH = pl.DeviceIdType.MESH
NN = (((1,), (0,)), ((), ()))
NT = (((1,), (1,)), ((), ()))
TN = (((0,), (0,)), ((), ()))


def mm(a, b, dims):
    return lax.dot_general(a, b, dims, preferred_element_type=F32)


def normalized(raw):
    rows, count = raw.shape
    vector = jnp.full((1, count), 1.0 / math.sqrt(count), F32)
    for _ in range(6):
        product = jnp.sum(raw * vector, axis=1, keepdims=True)
        returned = jnp.sum(raw * product, axis=0, keepdims=True)
        vector = returned / jnp.sqrt(jnp.sum(returned * returned, axis=1, keepdims=True))
    product = jnp.sum(raw * vector, axis=1, keepdims=True)
    return raw / jnp.sqrt(jnp.sum(product * product, axis=0, keepdims=True))


def kernel(
    n,
    nh,
    n_own,
    rows,
    q_ref,
    k_ref,
    v_ref,
    dy_ref,
    raw_ref,
    out_ref,
    gq_ref,
    gk_ref,
    gv_ref,
    gt_ref,
    u_src,
    u_all,
    m_src,
    m_all,
    s_src,
    s_all,
    av_acc,
    ady_acc,
    gqk_part,
    gqk_all,
    gt_part,
    gt_all,
    u_send,
    u_recv,
    m_send,
    m_recv,
    s_send,
    s_recv,
    h_send,
    h_recv,
):
    me = lax.axis_index("seq")
    core = lax.axis_index("head")
    tokens, states = q_ref.shape
    cols = v_ref.shape[1]
    heads_here = cols // P_SIZE
    scale = 0.5 / math.sqrt(STATE_ROWS * L)

    def peer(i):
        return lax.rem(me + i, n)

    def partner(i):
        return lax.rem(core + i, nh)

    barrier = pltpu.get_barrier_semaphore()

    def greet(i, carry):
        pl.semaphore_signal(
            barrier, inc=1, device_id={"seq": peer(i), "head": core}, device_id_type=MESH
        )
        return carry

    def greet_head(i, carry):
        pl.semaphore_signal(
            barrier, inc=1, device_id={"seq": me, "head": partner(i)}, device_id_type=MESH
        )
        return carry

    lax.fori_loop(1, n, greet, 0)
    lax.fori_loop(1, nh, greet_head, 0)

    q = q_ref[...]
    k = k_ref[...]
    u_src[0] = mm(v_ref[...], k, TN).astype(BF16)
    u_src[1] = (scale * mm(dy_ref[...], q, TN)).astype(BF16)

    pl.semaphore_wait(barrier, n - 1 + nh - 1)

    def when_owner(device):
        if n_own == n:
            return lambda body: body()
        return pl.when(device < n_own)

    def u_copy(target, source):
        return pltpu.make_async_remote_copy(
            src_ref=u_src.at[:, pl.ds(pl.multiple_of(target * rows, rows), rows)],
            dst_ref=u_all.at[source],
            send_sem=u_send.at[target],
            recv_sem=u_recv.at[source],
            device_id={"seq": target, "head": core},
            device_id_type=MESH,
        )

    def m_copy(target, source):
        return pltpu.make_async_remote_copy(
            src_ref=m_src,
            dst_ref=m_all.at[source],
            send_sem=m_send.at[target],
            recv_sem=m_recv.at[source],
            device_id={"seq": target, "head": core},
            device_id_type=MESH,
        )

    def s_copy(part, target, source):
        return pltpu.make_async_remote_copy(
            src_ref=s_src.at[part, target],
            dst_ref=s_all.at[part, pl.ds(pl.multiple_of(source * rows, rows), rows)],
            send_sem=s_send.at[part, target],
            recv_sem=s_recv.at[part, source],
            device_id={"seq": target, "head": core},
            device_id_type=MESH,
        )

    def send_u(i, carry):
        target = peer(i)

        @when_owner(target)
        def _():
            u_copy(target, me).start()

        return carry

    lax.fori_loop(1, n, send_u, 0)

    transition = normalized(raw_ref[0])
    eye = lax.broadcasted_iota(jnp.int32, (states, states), 0) == lax.broadcasted_iota(
        jnp.int32, (states, states), 1
    )
    diagonal = jnp.sum(jnp.where(eye, transition, 0.0), axis=0, keepdims=True)
    high = diagonal.astype(BF16).astype(F32)
    line = lax.broadcasted_iota(jnp.int32, (16, states), 0)
    m_src[0:states] = jnp.where(eye, 0.0, transition).astype(BF16)
    m_src[states : states + 16] = jnp.where(
        line == 0, high, jnp.where(line == 1, diagonal - high, 0.0)
    ).astype(BF16)

    def send_m(i, carry):
        target = peer(i)

        @when_owner(target)
        def _():
            m_copy(target, me).start()

        return carry

    lax.fori_loop(1, n, send_m, 0)

    @when_owner(me)
    def _():
        u_all[me] = u_src[:, pl.ds(pl.multiple_of(me * rows, rows), rows)]
        m_all[me] = m_src[...]

    causal = lax.broadcasted_iota(jnp.int32, (tokens, tokens), 0) >= lax.broadcasted_iota(
        jnp.int32, (tokens, tokens), 1
    )
    weights = jnp.where(causal, scale * mm(q, k, NT), 0.0).astype(BF16)
    av_acc[...] = mm(weights, v_ref[...], NN)
    ady_acc[...] = mm(weights, dy_ref[...], TN)
    gq = jnp.zeros((tokens, states), F32)
    gk = jnp.zeros((tokens, states), F32)
    for h in range(heads_here):
        span = slice(h * P_SIZE, (h + 1) * P_SIZE)
        dscore = mm(dy_ref[:, span], v_ref[:, span], NT)
        score_grad = jnp.where(causal, scale * dscore, 0.0).astype(BF16)
        gq += mm(score_grad, k, NN)
        gk += mm(score_grad, q, TN)
    gqk_part[0] = gq
    gqk_part[1] = gk

    def split(x):
        top = x.astype(BF16)
        return top, jnp.concatenate([top, (x - top.astype(F32)).astype(BF16)], axis=0)

    def step(lap, carry):
        x, y = carry
        late = n - 1 - lap
        x_low, x_pair = split(x)
        y_low, y_pair = split(y)
        s_src[0, lap] = x_low
        s_src[1, late] = y_low

        @pl.when(lap != me)
        def _():
            s_copy(0, lap, me).start()

        @pl.when(late != me)
        def _():
            s_copy(1, late, me).start()

        def diag(at):
            tail = m_all[at, states : states + 16].astype(F32)
            return tail[0:1] + tail[1:2]

        x_wide = mm(x_pair, m_all[lap, 0:states], NT)
        y_wide = mm(y_pair, m_all[late, 0:states], NN)
        x = x_wide[0:rows] + x_wide[rows:] + x * diag(lap) + u_all[lap, 0].astype(F32)
        y = y_wide[0:rows] + y_wide[rows:] + y * diag(late) + u_all[late, 1].astype(F32)
        return x, y

    @when_owner(me)
    def _():
        def arrive(i, carry):
            source = peer(i)
            u_copy(me, source).wait_recv()
            m_copy(me, source).wait_recv()
            return carry

        lax.fori_loop(1, n, arrive, 0)
        zero = jnp.zeros((rows, states), F32)
        lax.fori_loop(0, n, step, (zero, zero))
        own = pl.ds(pl.multiple_of(me * rows, rows), rows)
        s_all[0, own] = s_src[0, me]
        s_all[1, own] = s_src[1, me]

    def collect(i, carry):
        source = peer(i)

        @when_owner(source)
        def _():
            s_copy(0, me, source).wait_recv()
            s_copy(1, me, source).wait_recv()

        return carry

    lax.fori_loop(1, n, collect, 0)

    state_t = s_all[0]
    grad_t = s_all[1]
    gqk_part[0] += scale * mm(dy_ref[...], state_t, NN)
    gqk_part[1] += mm(v_ref[...], grad_t, NN)
    gt_part[...] = mm(grad_t, state_t, TN)

    share = tokens // nh
    row_share = states // nh

    def qk_copy(target, source):
        return pltpu.make_async_remote_copy(
            src_ref=gqk_part.at[:, pl.ds(pl.multiple_of(target * share, share), share)],
            dst_ref=gqk_all.at[source],
            send_sem=h_send.at[0, target],
            recv_sem=h_recv.at[0, source],
            device_id={"seq": me, "head": target},
            device_id_type=MESH,
        )

    def gt_copy(target, source):
        return pltpu.make_async_remote_copy(
            src_ref=gt_part.at[pl.ds(pl.multiple_of(target * row_share, row_share), row_share)],
            dst_ref=gt_all.at[source],
            send_sem=h_send.at[1, target],
            recv_sem=h_recv.at[1, source],
            device_id={"seq": me, "head": target},
            device_id_type=MESH,
        )

    def send_heads(i, carry):
        qk_copy(partner(i), core).start()
        gt_copy(partner(i), core).start()
        return carry

    lax.fori_loop(1, nh, send_heads, 0)

    out_ref[...] = (av_acc[...] + scale * mm(q, state_t, NT)).astype(BF16)
    gv_ref[...] = (ady_acc[...] + mm(k, grad_t, NT)).astype(BF16)

    own_share = pl.ds(pl.multiple_of(core * share, share), share)
    own_rows = pl.ds(pl.multiple_of(core * row_share, row_share), row_share)

    def add_heads(i, carry):
        gq_sum, gk_sum, gt_sum = carry
        source = partner(i)
        qk_copy(core, source).wait_recv()
        gt_copy(core, source).wait_recv()
        return (
            gq_sum + gqk_all[source, 0],
            gk_sum + gqk_all[source, 1],
            gt_sum + gt_all[source],
        )

    sums = (gqk_part[0, own_share], gqk_part[1, own_share], gt_part[own_rows])
    for i in range(1, nh):
        sums = add_heads(i, sums)
    gq_ref[...] = sums[0].astype(BF16)
    gk_ref[...] = sums[1].astype(BF16)
    gt_ref[...] = sums[2]

    def drain(i, carry):
        target = peer(i)

        @when_owner(target)
        def _():
            u_copy(target, me).wait_send()
            m_copy(target, me).wait_send()

        @when_owner(me)
        def _():
            s_copy(0, target, me).wait_send()
            s_copy(1, target, me).wait_send()

        return carry

    lax.fori_loop(1, n, drain, 0)

    def drain_heads(i, carry):
        qk_copy(partner(i), core).wait_send()
        gt_copy(partner(i), core).wait_send()
        return carry

    lax.fori_loop(1, nh, drain_heads, 0)


def per_device(queries, keys, values, out_grad, raw_trans):
    n = lax.axis_size("seq")
    nh = lax.axis_size("head")
    assert raw_trans.shape[0] == 1
    tokens, states = queries.shape
    cols = values.shape[1]
    rows = max(16, cols // n)
    n_own = cols // rows
    share = tokens // nh
    row_share = states // nh
    vmem = pl.BlockSpec(memory_space=pltpu.VMEM)
    outs = pl.pallas_call(
        functools.partial(kernel, n, nh, n_own, rows),
        out_shape=(
            jax.ShapeDtypeStruct((tokens, cols), BF16),
            jax.ShapeDtypeStruct((share, states), BF16),
            jax.ShapeDtypeStruct((share, states), BF16),
            jax.ShapeDtypeStruct((tokens, cols), BF16),
            jax.ShapeDtypeStruct((row_share, states), F32),
        ),
        in_specs=[vmem] * 5,
        out_specs=(vmem,) * 5,
        scratch_shapes=[
            pltpu.VMEM((2, cols, states), BF16),
            pltpu.VMEM((n, 2, rows, states), BF16),
            pltpu.VMEM((states + 16, states), BF16),
            pltpu.VMEM((n, states + 16, states), BF16),
            pltpu.VMEM((2, n, rows, states), BF16),
            pltpu.VMEM((2, cols, states), BF16),
            pltpu.VMEM((tokens, cols), F32),
            pltpu.VMEM((tokens, cols), F32),
            pltpu.VMEM((2, tokens, states), F32),
            pltpu.VMEM((nh, 2, share, states), F32),
            pltpu.VMEM((states, states), F32),
            pltpu.VMEM((nh, row_share, states), F32),
            pltpu.SemaphoreType.DMA((n,)),
            pltpu.SemaphoreType.DMA((n,)),
            pltpu.SemaphoreType.DMA((n,)),
            pltpu.SemaphoreType.DMA((n,)),
            pltpu.SemaphoreType.DMA((2, n)),
            pltpu.SemaphoreType.DMA((2, n)),
            pltpu.SemaphoreType.DMA((2, nh)),
            pltpu.SemaphoreType.DMA((2, nh)),
        ],
        compiler_params=pltpu.CompilerParams(
            collective_id=0, has_side_effects=True, vmem_limit_bytes=40 * 1024 * 1024
        ),
    )(queries, keys, values, out_grad, raw_trans)
    out, gq, gk, gv, gt = outs
    return out, gq, gk, gv, gt.reshape(row_share, 1, states)


def solution(mesh):
    in_specs = (
        P("seq", None),
        P("seq", None),
        P("seq", "head"),
        P("seq", "head"),
        P("seq", None, None),
    )
    out_specs = (
        P("seq", "head"),
        P(("seq", "head"), None),
        P(("seq", "head"), None),
        P("seq", "head"),
        P("head", "seq", None),
    )
    return jax.shard_map(
        per_device, mesh=mesh, in_specs=in_specs, out_specs=out_specs, check_vma=False
    )
```

time: 432 us -> 60.5 us (0.14)
  waiting for transfers between devices: 342 us -> 0 us
  matrix products: 61 us -> 0 us
  Pallas kernels: 0 us -> 51.4 us
  between operations: 19.1 us -> 0.66 us
  local copies, waits for them, and re-layouts: 3.18 us -> 8.02 us
  blocking collectives: 4.48 us -> 0 us
    all_gather x4 -> x0, waiting for transfers between devices: 304 us -> none  [prefix(): gathered = jax.tree.map(lambda a: lax.all_gather(a, axis), part)]
    dot_general x45 -> x0, matrix products: 61 us -> none  [the longest x17 27.4 us: compose(): jnp.dot(matrix_late, vector_early, precision=PRECISE) + vector_late]
    pallas_call x0 -> x1, Pallas kernels: none -> 51.4 us  [per_device(): pl.pallas_call(functools.partial(kernel, n, nh, n_own, rows), out_shape=(...]
    unnamed x8 -> x0, waiting for transfers between devices: 38.1 us -> none
    unnamed x11 -> x15, local copies, waits for them, and re-layouts: 2.48 us -> 8.02 us
    all_gather x2 -> x0, blocking collectives: 4.48 us -> none  [the longest x1 2.31 us: per_device(): grad_piece = lax.all_gather(carried_lows, 'head', axis=2, tiled=True)]
  transfers between devices with their start and end apart: 6 -> 0, of which waited for: 6 -> 0; matrix products, arithmetic and copies ran while one was open for 9% -> 0% of each run, Pallas kernels for 0% -> 0%
where the time goes in v1:
time: 60.5 us; the launch traced here: 60 us
  Pallas kernels  51.4 us (85%)
  local copies, waits for them, and re-layouts  8.02 us (13%)
  between operations  0.66 us (1%)
    pallas_call x1, Pallas kernels, per_device(): pl.pallas_call(functools.partial(kernel, n, nh, n_own, rows), out_shape=(...  51.4 us
    unnamed x15, local copies, waits for them, and re-layouts  8.02 us

profile of v1, /device:TPU:0, one launch (start us, length us, event | category | flops | bytes accessed | tf_op | source)
XLA Modules:
  0.0 60.0 jit_solution(194721859855311437)
XLA Ops:
  0.6 0.0 copy-start
  0.6 1.0 %copy-done = bf16[256,1024]{1,0:T(8,128)(2,1)S(1)} copy-done((bf16[256,1024]{1,0:T(8,128)(2,1)S(1)}, bf16[256,1024]{1,0:T(8,128)(2,1)}, u32[]{:S(2)}) %copy-start) | copy-done | bytes 524312
  1.7 0.0 copy-start.1
  1.7 1.0 %copy-done.1 = bf16[256,1024]{1,0:T(8,128)(2,1)S(1)} copy-done((bf16[256,1024]{1,0:T(8,128)(2,1)S(1)}, bf16[256,1024]{1,0:T(8,128)(2,1)}, u32[]{:S(2)}) %copy-start.1) | copy-done | bytes 524312
  2.7 0.0 copy-start.2
  2.7 0.8 %copy-done.2 = bf16[256,128]{1,0:T(8,128)(2,1)S(1)} copy-done((bf16[256,128]{1,0:T(8,128)(2,1)S(1)}, bf16[256,128]{1,0:T(8,128)(2,1)}, u32[]{:S(2)}) %copy-start.2) | copy-done | bytes 65560
  3.6 0.0 copy-start.3
  3.6 0.8 %copy-done.3 = bf16[256,128]{1,0:T(8,128)(2,1)S(1)} copy-done((bf16[256,128]{1,0:T(8,128)(2,1)S(1)}, bf16[256,128]{1,0:T(8,128)(2,1)}, u32[]{:S(2)}) %copy-start.3) | copy-done | bytes 65560
  4.4 0.0 copy-start.4
  4.4 0.8 %copy-done.4 = f32[1,128,128]{2,1,0:T(8,128)S(1)} copy-done((f32[1,128,128]{2,1,0:T(8,128)S(1)}, f32[1,128,128]{2,1,0:T(8,128)}, u32[]{:S(2)}) %copy-start.4) | copy-done | bytes 65560
  5.2 51.4 %shard_map.92 = (bf16[256,1024]{1,0:T(8,128)(2,1)S(1)}, bf16[128,128]{1,0:T(8,128)(2,1)S(1)}, bf16[128,128]{1,0:T(8,128)(2,1)S(1)}, bf16[256,1024]{1,0:T(8,128)(2,1)S(1)}, f32[64,128]{1,0:T(8,128)S(1)}) custom-call(bf16[256,128]{1,0:T(8,128)(2,1)S(1)} %copy-done.2, bf16[256,128]{1,0:T(8,128)(2,1)S(1)} %copy-done.3, bf16[256,1024]{1,0:T(8,128)(2,1)S(1)} %copy-done, ...), custom_call_target="tpu_custom_call" | custom-call | tf_op jit(solution)/shard_map/pallas_call | solution.py:355
  56.6 0.8 %copy.16 = bf16[256,1024]{1,0:T(8,128)(2,1)} copy(bf16[256,1024]{1,0:T(8,128)(2,1)S(1)} %get-tuple-element.25) | data formatting | bytes 1048576
  57.4 0.6 %copy.17 = bf16[128,128]{1,0:T(8,128)(2,1)} copy(bf16[128,128]{1,0:T(8,128)(2,1)S(1)} %get-tuple-element.26) | data formatting | bytes 65536
  58.0 0.6 %copy.18 = bf16[128,128]{1,0:T(8,128)(2,1)} copy(bf16[128,128]{1,0:T(8,128)(2,1)S(1)} %get-tuple-element.27) | data formatting | bytes 65536
  58.6 0.8 %copy.19 = bf16[256,1024]{1,0:T(8,128)(2,1)} copy(bf16[256,1024]{1,0:T(8,128)(2,1)S(1)} %get-tuple-element.28) | data formatting | bytes 1048576
  59.4 0.6 %copy.20 = f32[64,1,128]{2,1,0:T(1,128)} copy(f32[64,1,128]{2,1,0:T(1,128)S(1)} %bitcast.3) | data formatting | bytes 65536
Async XLA Ops:
  0.6 1.0 %copy-start = (bf16[256,1024]{1,0:T(8,128)(2,1)S(1)}, bf16[256,1024]{1,0:T(8,128)(2,1)}, u32[]{:S(2)}) copy-start(bf16[256,1024]{1,0:T(8,128)(2,1)} %v_ref.1) | copy-start | bytes 1572868
  1.7 1.0 %copy-start.1 = (bf16[256,1024]{1,0:T(8,128)(2,1)S(1)}, bf16[256,1024]{1,0:T(8,128)(2,1)}, u32[]{:S(2)}) copy-start(bf16[256,1024]{1,0:T(8,128)(2,1)} %dy_ref.1) | copy-start | bytes 1572868
  2.7 0.8 %copy-start.2 = (bf16[256,128]{1,0:T(8,128)(2,1)S(1)}, bf16[256,128]{1,0:T(8,128)(2,1)}, u32[]{:S(2)}) copy-start(bf16[256,128]{1,0:T(8,128)(2,1)} %q_ref.1) | copy-start | bytes 196612
  3.6 0.8 %copy-start.3 = (bf16[256,128]{1,0:T(8,128)(2,1)S(1)}, bf16[256,128]{1,0:T(8,128)(2,1)}, u32[]{:S(2)}) copy-start(bf16[256,128]{1,0:T(8,128)(2,1)} %k_ref.1) | copy-start | bytes 196612
  4.4 0.8 %copy-start.4 = (f32[1,128,128]{2,1,0:T(8,128)S(1)}, f32[1,128,128]{2,1,0:T(8,128)}, u32[]{:S(2)}) copy-start(f32[1,128,128]{2,1,0:T(8,128)} %raw_ref.1) | copy-start | bytes 196612

commit v2 on v1

v2 whole, which is shorter than its diff:
```python
import functools
import math

import jax
import jax.numpy as jnp
from jax import lax
from jax.experimental import pallas as pl
from jax.experimental.pallas import tpu as pltpu
from jax.sharding import PartitionSpec as P

STATE_ROWS = 128
P_SIZE = 256
L = 256

F32 = jnp.float32
BF16 = jnp.bfloat16
MESH = pl.DeviceIdType.MESH
NN = (((1,), (0,)), ((), ()))
NT = (((1,), (1,)), ((), ()))
TN = (((0,), (0,)), ((), ()))


def mm(a, b, dims):
    return lax.dot_general(a, b, dims, preferred_element_type=F32)


def normalized(raw):
    rows, count = raw.shape
    vector = jnp.full((1, count), 1.0 / math.sqrt(count), F32)
    for _ in range(6):
        product = jnp.sum(raw * vector, axis=1, keepdims=True)
        returned = jnp.sum(raw * product, axis=0, keepdims=True)
        vector = returned / jnp.sqrt(jnp.sum(returned * returned, axis=1, keepdims=True))
    product = jnp.sum(raw * vector, axis=1, keepdims=True)
    return raw / jnp.sqrt(jnp.sum(product * product, axis=0, keepdims=True))


def split(x):
    top = x.astype(BF16)
    return top, (x - top.astype(F32)).astype(BF16)


def kernel(
    n,
    nh,
    group,
    chunks,
    q_hbm,
    k_hbm,
    v_hbm,
    dy_hbm,
    raw_hbm,
    out_ref,
    gq_ref,
    gk_ref,
    gv_ref,
    gt_ref,
    q_ref,
    k_ref,
    v_ref,
    dy_ref,
    raw_ref,
    u_src,
    u_all,
    m_src,
    m_all,
    e_src,
    e_all,
    tail_acc,
    s_src,
    s_all,
    av_acc,
    ady_acc,
    gqk_part,
    gqk_all,
    gt_part,
    gt_all,
    in_sem,
    u_send,
    u_recv,
    m_send,
    m_recv,
    e_send,
    e_recv,
    s_send,
    s_recv,
    h_send,
    h_recv,
):
    me = lax.axis_index("seq")
    core = lax.axis_index("head")
    place = lax.rem(me, group)
    plane = lax.div(me, group)
    planes = n // group
    half = planes // 2
    tokens, states = q_ref.shape
    cols = v_ref.shape[1]
    rows = cols // group
    piece = rows // chunks
    heads_here = cols // P_SIZE
    scale = 0.5 / math.sqrt(STATE_ROWS * L)

    def load(index, source, target):
        return pltpu.make_async_copy(source, target, in_sem.at[index])

    loads = [
        load(i, source, target)
        for i, (source, target) in enumerate(
            (
                (raw_hbm, raw_ref),
                (q_hbm, q_ref),
                (k_hbm, k_ref),
                (v_hbm, v_ref),
                (dy_hbm, dy_ref),
            )
        )
    ]
    for copy in loads:
        copy.start()

    def mate(i):
        return lax.rem(place + i, group)

    def partner(i):
        return lax.rem(core + i, nh)

    def at_place(j):
        return {"seq": plane * group + j, "head": core}

    def at_plane(z):
        return {"seq": z * group + place, "head": core}

    barrier = pltpu.get_barrier_semaphore()

    def signal(device):
        pl.semaphore_signal(barrier, inc=1, device_id=device, device_id_type=MESH)

    for i in range(1, group):
        signal(at_place(mate(i)))
    for i in range(1, nh):
        signal({"seq": me, "head": partner(i)})

    @pl.when(plane > 0)
    def _():
        signal(at_plane(plane - 1))

    @pl.when(plane < planes - 1)
    def _():
        signal(at_plane(plane + 1))

    for copy in loads:
        copy.wait()

    q = q_ref[...]
    k = k_ref[...]
    u_src[0] = mm(v_ref[...], k, TN).astype(BF16)
    u_src[1] = (scale * mm(dy_ref[...], q, TN)).astype(BF16)
    transition = normalized(raw_ref[0])
    eye = lax.broadcasted_iota(jnp.int32, (states, states), 0) == lax.broadcasted_iota(
        jnp.int32, (states, states), 1
    )
    diagonal = jnp.sum(jnp.where(eye, transition, 0.0), axis=0, keepdims=True)
    high = diagonal.astype(BF16).astype(F32)
    line = lax.broadcasted_iota(jnp.int32, (16, states), 0)
    m_src[0:states] = jnp.where(eye, 0.0, transition).astype(BF16)
    m_src[states : states + 16] = jnp.where(
        line == 0, high, jnp.where(line == 1, diagonal - high, 0.0)
    ).astype(BF16)

    above = lax.min(plane, 1)
    below = lax.min(planes - 1 - plane, 1)
    pl.semaphore_wait(barrier, group - 1 + nh - 1 + above + below)

    def slab(j):
        return pl.ds(pl.multiple_of(j * rows, rows), rows)

    def u_copy(target, source):
        return pltpu.make_async_remote_copy(
            src_ref=u_src.at[:, slab(target)],
            dst_ref=u_all.at[source],
            send_sem=u_send.at[target],
            recv_sem=u_recv.at[source],
            device_id=at_place(target),
            device_id_type=MESH,
        )

    def m_copy(target, source):
        return pltpu.make_async_remote_copy(
            src_ref=m_src,
            dst_ref=m_all.at[source],
            send_sem=m_send.at[target],
            recv_sem=m_recv.at[source],
            device_id=at_place(target),
            device_id_type=MESH,
        )

    def e_copy(part, chunk, target):
        span = pl.ds(chunk * piece, piece)
        return pltpu.make_async_remote_copy(
            src_ref=e_src.at[part, span],
            dst_ref=e_all.at[part, span],
            send_sem=e_send.at[part, chunk],
            recv_sem=e_recv.at[part, chunk],
            device_id=at_plane(target),
            device_id_type=MESH,
        )

    def s_copy(part, target, source):
        return pltpu.make_async_remote_copy(
            src_ref=s_src.at[part, target],
            dst_ref=s_all.at[part, slab(source)],
            send_sem=s_send.at[part, target],
            recv_sem=s_recv.at[part, source],
            device_id=at_place(target),
            device_id_type=MESH,
        )

    for i in range(1, group):
        m_copy(mate(i), place).start()
    for i in range(1, group):
        u_copy(mate(i), place).start()
    u_all[place] = u_src[:, slab(place)]
    m_all[place] = m_src[...]

    causal = lax.broadcasted_iota(jnp.int32, (tokens, tokens), 0) >= lax.broadcasted_iota(
        jnp.int32, (tokens, tokens), 1
    )
    weights = jnp.where(causal, scale * mm(q, k, NT), 0.0).astype(BF16)
    av_acc[...] = mm(weights, v_ref[...], NN)
    ady_acc[...] = mm(weights, dy_ref[...], TN)
    gq = jnp.zeros((tokens, states), F32)
    gk = jnp.zeros((tokens, states), F32)
    for h in range(heads_here):
        span = slice(h * P_SIZE, (h + 1) * P_SIZE)
        dscore = mm(dy_ref[:, span], v_ref[:, span], NT)
        score_grad = jnp.where(causal, scale * dscore, 0.0).astype(BF16)
        gq += mm(score_grad, k, NN)
        gk += mm(score_grad, q, TN)
    gqk_part[0] = gq
    gqk_part[1] = gk

    for i in range(1, group):
        m_copy(place, mate(i)).wait_recv()
    for i in range(1, group):
        u_copy(place, mate(i)).wait_recv()

    def advance(x, j, dims):
        count = x.shape[0]
        tail = m_all[j, states : states + 16].astype(F32)
        wide = mm(jnp.concatenate(split(x), axis=0), m_all[j, 0:states], dims)
        return wide[0:count] + wide[count:] + x * (tail[0:1] + tail[1:2])

    x = jnp.concatenate(
        [jnp.zeros((rows, states), F32), jnp.where(eye, 1.0, 0.0).astype(F32)], axis=0
    )
    y = jnp.zeros((rows, states), F32)
    for lap in range(group):
        late = group - 1 - lap
        if lap == 0:
            x_rows = u_all[0, 0].astype(F32)
            y = u_all[late, 1].astype(F32)
            product = advance(x[rows:], 0, NT)
        else:
            x = advance(jnp.concatenate([x_rows, product], axis=0), lap, NT)
            x_rows = x[0:rows] + u_all[lap, 0].astype(F32)
            product = x[rows:]
            y = advance(y, late, NN) + u_all[late, 1].astype(F32)
    tail_acc[0] = x_rows
    tail_acc[1] = y
    top, rest = split(product)
    spread = (jnp.concatenate([top, rest], axis=0), jnp.concatenate([top, rest], axis=1))

    def run(part):
        first = (plane == 0, plane == planes - 1)[part]
        final = (plane == planes - 1, plane == 0)[part]
        towards = (plane + 1, plane - 1)[part]
        dims = (NN, NT)[part]

        @pl.when(first)
        def _():
            e_src[part] = tail_acc[part].astype(BF16)
            e_all[part] = jnp.zeros((rows, states), BF16)
            if planes > 1:
                for chunk in range(chunks):
                    e_copy(part, chunk, towards).start()

        @pl.when(jnp.logical_not(first))
        def _():
            for chunk in range(chunks):
                e_copy(part, chunk, plane).wait_recv()

                @pl.when(jnp.logical_not(final))
                def _():
                    span = pl.ds(chunk * piece, piece)
                    entered = e_all[part, span]
                    left = mm(jnp.concatenate([entered, entered], axis=1), spread[part], dims)
                    e_src[part, span] = (left + tail_acc[part, span]).astype(BF16)
                    e_copy(part, chunk, towards).start()

        state = e_all[part].astype(F32)
        for lap in range(group):
            j = (lap, group - 1 - lap)[part]
            s_src[part, j] = state.astype(BF16)

            @pl.when(place != j)
            def _():
                s_copy(part, j, place).start()

            @pl.when(place == j)
            def _():
                s_all[part, slab(place)] = s_src[part, j]

            if lap < group - 1:
                state = advance(state, j, (NT, NN)[part]) + u_all[j, part].astype(F32)

    def collect(part):
        for i in range(1, group):
            s_copy(part, place, mate(i)).wait_recv()

    share = tokens // nh
    row_share = states // nh

    def qk_copy(target, source):
        return pltpu.make_async_remote_copy(
            src_ref=gqk_part.at[:, pl.ds(pl.multiple_of(target * share, share), share)],
            dst_ref=gqk_all.at[source],
            send_sem=h_send.at[0, target],
            recv_sem=h_recv.at[0, source],
            device_id={"seq": me, "head": target},
            device_id_type=MESH,
        )

    def gt_copy(target, source):
        return pltpu.make_async_remote_copy(
            src_ref=gt_part.at[pl.ds(pl.multiple_of(target * row_share, row_share), row_share)],
            dst_ref=gt_all.at[source],
            send_sem=h_send.at[1, target],
            recv_sem=h_recv.at[1, source],
            device_id={"seq": me, "head": target},
            device_id_type=MESH,
        )

    def small(part):
        if part == 0:
            gqk_part[0] += scale * mm(dy_ref[...], s_all[0], NN)
        else:
            gqk_part[1] += mm(v_ref[...], s_all[1], NN)

    def large(part):
        if part == 0:
            out_ref[...] = (av_acc[...] + scale * mm(q_ref[...], s_all[0], NT)).astype(BF16)
        else:
            gv_ref[...] = (ady_acc[...] + mm(k_ref[...], s_all[1], NT)).astype(BF16)

    def whole(part):
        other = 1 - part
        run(part)
        run(other)
        collect(part)
        small(part)
        large(part)
        collect(other)
        small(other)
        gt_part[...] = mm(s_all[1], s_all[0], TN)
        for i in range(1, nh):
            qk_copy(partner(i), core).start()
            gt_copy(partner(i), core).start()
        large(other)

    @pl.when(plane < half)
    def _():
        whole(0)

    @pl.when(plane >= half)
    def _():
        whole(1)

    own_share = pl.ds(pl.multiple_of(core * share, share), share)
    own_rows = pl.ds(pl.multiple_of(core * row_share, row_share), row_share)
    gq_sum = gqk_part[0, own_share]
    gk_sum = gqk_part[1, own_share]
    gt_sum = gt_part[own_rows]
    for i in range(1, nh):
        source = partner(i)
        qk_copy(core, source).wait_recv()
        gt_copy(core, source).wait_recv()
        gq_sum += gqk_all[source, 0]
        gk_sum += gqk_all[source, 1]
        gt_sum += gt_all[source]
    gq_ref[...] = gq_sum.astype(BF16)
    gk_ref[...] = gk_sum.astype(BF16)
    gt_ref[...] = gt_sum

    for i in range(1, group):
        target = mate(i)
        u_copy(target, place).wait_send()
        m_copy(target, place).wait_send()
        s_copy(0, target, place).wait_send()
        s_copy(1, target, place).wait_send()
    for i in range(1, nh):
        qk_copy(partner(i), core).wait_send()
        gt_copy(partner(i), core).wait_send()

    @pl.when(plane < planes - 1)
    def _():
        for chunk in range(chunks):
            e_copy(0, chunk, plane + 1).wait_send()

    @pl.when(plane > 0)
    def _():
        for chunk in range(chunks):
            e_copy(1, chunk, plane - 1).wait_send()


def store(*refs):
    count = len(refs) // 2
    sem = refs[-1]
    copies = [
        pltpu.make_async_copy(refs[i], refs[count + i], sem.at[i]) for i in range(count)
    ]
    for copy in copies:
        copy.start()
    for copy in copies:
        copy.wait()


def per_device(queries, keys, values, out_grad, raw_trans):
    n = lax.axis_size("seq")
    nh = lax.axis_size("head")
    assert raw_trans.shape[0] == 1
    tokens, states = queries.shape
    cols = values.shape[1]
    group = math.gcd(n, 4)
    rows = cols // group
    chunks = 2
    share = tokens // nh
    row_share = states // nh
    vmem = pl.BlockSpec(memory_space=pltpu.VMEM)
    anywhere = pl.BlockSpec(memory_space=pltpu.HBM)
    shapes = (
        jax.ShapeDtypeStruct((tokens, cols), BF16),
        jax.ShapeDtypeStruct((share, states), BF16),
        jax.ShapeDtypeStruct((share, states), BF16),
        jax.ShapeDtypeStruct((tokens, cols), BF16),
        jax.ShapeDtypeStruct((row_share, states), F32),
    )
    queries, keys, values, out_grad, raw_trans = (
        pltpu.with_memory_space_constraint(x, pltpu.HBM)
        for x in (queries, keys, values, out_grad, raw_trans)
    )
    outs = pl.pallas_call(
        functools.partial(kernel, n, nh, group, chunks),
        out_shape=shapes,
        in_specs=[anywhere] * 5,
        out_specs=(vmem,) * 5,
        scratch_shapes=[
            pltpu.VMEM((tokens, states), BF16),
            pltpu.VMEM((tokens, states), BF16),
            pltpu.VMEM((tokens, cols), BF16),
            pltpu.VMEM((tokens, cols), BF16),
            pltpu.VMEM((1, states, states), F32),
            pltpu.VMEM((2, cols, states), BF16),
            pltpu.VMEM((group, 2, rows, states), BF16),
            pltpu.VMEM((states + 16, states), BF16),
            pltpu.VMEM((group, states + 16, states), BF16),
            pltpu.VMEM((2, rows, states), BF16),
            pltpu.VMEM((2, rows, states), BF16),
            pltpu.VMEM((2, rows, states), F32),
            pltpu.VMEM((2, group, rows, states), BF16),
            pltpu.VMEM((2, cols, states), BF16),
            pltpu.VMEM((tokens, cols), F32),
            pltpu.VMEM((tokens, cols), F32),
            pltpu.VMEM((2, tokens, states), F32),
            pltpu.VMEM((nh, 2, share, states), F32),
            pltpu.VMEM((states, states), F32),
            pltpu.VMEM((nh, row_share, states), F32),
            pltpu.SemaphoreType.DMA((5,)),
            pltpu.SemaphoreType.DMA((group,)),
            pltpu.SemaphoreType.DMA((group,)),
            pltpu.SemaphoreType.DMA((group,)),
            pltpu.SemaphoreType.DMA((group,)),
            pltpu.SemaphoreType.DMA((2, chunks)),
            pltpu.SemaphoreType.DMA((2, chunks)),
            pltpu.SemaphoreType.DMA((2, group)),
            pltpu.SemaphoreType.DMA((2, group)),
            pltpu.SemaphoreType.DMA((2, nh)),
            pltpu.SemaphoreType.DMA((2, nh)),
        ],
        compiler_params=pltpu.CompilerParams(
            collective_id=0, has_side_effects=True, vmem_limit_bytes=32 * 1024 * 1024
        ),
    )(queries, keys, values, out_grad, raw_trans)
    out, gq, gk, gv, gt = pl.pallas_call(
        store,
        out_shape=shapes,
        in_specs=[vmem] * 5,
        out_specs=(anywhere,) * 5,
        scratch_shapes=[pltpu.SemaphoreType.DMA((5,))],
        compiler_params=pltpu.CompilerParams(vmem_limit_bytes=4 * 1024 * 1024),
    )(*outs)
    return out, gq, gk, gv, gt.reshape(row_share, 1, states)


def solution(mesh):
    in_specs = (
        P("seq", None),
        P("seq", None),
        P("seq", "head"),
        P("seq", "head"),
        P("seq", None, None),
    )
    out_specs = (
        P("seq", "head"),
        P(("seq", "head"), None),
        P(("seq", "head"), None),
        P("seq", "head"),
        P("head", "seq", None),
    )
    return jax.shard_map(
        per_device, mesh=mesh, in_specs=in_specs, out_specs=out_specs, check_vma=False
    )
```

time: 60.5 us -> 34.1 us (0.56)
  Pallas kernels: 51.4 us -> 33.3 us
  local copies, waits for them, and re-layouts: 8.02 us -> 0 us
    pallas_call x1 -> x2, Pallas kernels: 51.4 us -> 33.3 us  [the longest x1 32.3 us: per_device(): pl.pallas_call(functools.partial(kernel, n, nh, group, chunks), out_shape...]
    unnamed x15 -> x0, local copies, waits for them, and re-layouts: 8.02 us -> none
where the time goes in v2:
time: 34.1 us; the launch traced here: 34 us
  Pallas kernels  33.3 us (98%)
  between operations  0.64 us (2%)
    pallas_call x1, Pallas kernels, per_device(): pl.pallas_call(functools.partial(kernel, n, nh, group, chunks), out_shape...  32.3 us
    pallas_call x1, Pallas kernels, per_device(): pl.pallas_call(store, out_shape=shapes, in_specs=[vmem] * 5, out_specs=(a...  1.04 us

profile of v2, /device:TPU:0, one launch (start us, length us, event | category | flops | bytes accessed | tf_op | source)
XLA Modules:
  0.0 34.0 jit_solution(11971255840585122892)
XLA Ops:
  0.6 32.3 %shard_map.92 = (bf16[256,1024]{1,0:T(8,128)(2,1)S(1)}, bf16[128,128]{1,0:T(8,128)(2,1)S(1)}, bf16[128,128]{1,0:T(8,128)(2,1)S(1)}, bf16[256,1024]{1,0:T(8,128)(2,1)S(1)}, f32[64,128]{1,0:T(8,128)S(1)}) custom-call(bf16[256,128]{1,0:T(8,128)(2,1)} %q_hbm.1, bf16[256,128]{1,0:T(8,128)(2,1)} %k_hbm.1, bf16[256,1024]{1,0:T(8,128)(2,1)} %v_hbm.1, ...), custom_call_target="tpu_custom_call" | custom-call | tf_op jit(solution)/shard_map/pallas_call | solution.py:451
  32.9 1.0 %shard_map.93 = (bf16[256,1024]{1,0:T(8,128)(2,1)}, bf16[128,128]{1,0:T(8,128)(2,1)}, bf16[128,128]{1,0:T(8,128)(2,1)}, bf16[256,1024]{1,0:T(8,128)(2,1)}, f32[64,128]{1,0:T(8,128)}) custom-call(bf16[256,1024]{1,0:T(8,128)(2,1)S(1)} %get-tuple-element.15.refs_0_, bf16[128,128]{1,0:T(8,128)(2,1)S(1)} %get-tuple-element.16.refs_1_, ...), custom_call_target="tpu_custom_call" | custom-call | tf_op jit(solution)/shard_map/pallas_call | solution.py:493

commit v3 on v2

--- a/solution.py
+++ b/solution.py
@@ -66,7 +66,8 @@
     m_all,
     e_src,
     e_all,
-    tail_acc,
+    prod,
+    local,
     s_src,
     s_all,
     av_acc,
@@ -174,12 +175,15 @@
     def slab(j):
         return pl.ds(pl.multiple_of(j * rows, rows), rows)
 
-    def u_copy(target, source):
+    def bit(j, chunk):
+        return pl.ds(pl.multiple_of(j * rows + chunk * piece, piece), piece)
+
+    def u_copy(chunk, target, source):
         return pltpu.make_async_remote_copy(
-            src_ref=u_src.at[:, slab(target)],
-            dst_ref=u_all.at[source],
-            send_sem=u_send.at[target],
-            recv_sem=u_recv.at[source],
+            src_ref=u_src.at[:, bit(target, chunk)],
+            dst_ref=u_all.at[source, :, pl.ds(chunk * piece, piece)],
+            send_sem=u_send.at[chunk, target],
+            recv_sem=u_recv.at[chunk, source],
             device_id=at_place(target),
             device_id_type=MESH,
         )
@@ -205,20 +209,21 @@
             device_id_type=MESH,
         )
 
-    def s_copy(part, target, source):
+    def s_copy(part, chunk, target, source):
         return pltpu.make_async_remote_copy(
-            src_ref=s_src.at[part, target],
-            dst_ref=s_all.at[part, slab(source)],
-            send_sem=s_send.at[part, target],
-            recv_sem=s_recv.at[part, source],
+            src_ref=s_src.at[part, target, pl.ds(chunk * piece, piece)],
+            dst_ref=s_all.at[part, bit(source, chunk)],
+            send_sem=s_send.at[part, chunk, target],
+            recv_sem=s_recv.at[part, chunk, source],
             device_id=at_place(target),
             device_id_type=MESH,
         )
 
     for i in range(1, group):
         m_copy(mate(i), place).start()
-    for i in range(1, group):
-        u_copy(mate(i), place).start()
+    for chunk in range(chunks):
+        for i in range(1, group):
+            u_copy(chunk, mate(i), place).start()
     u_all[place] = u_src[:, slab(place)]
     m_all[place] = m_src[...]
 
@@ -241,81 +246,97 @@
 
     for i in range(1, group):
         m_copy(place, mate(i)).wait_recv()
-    for i in range(1, group):
-        u_copy(place, mate(i)).wait_recv()
-
     def advance(x, j, dims):
         count = x.shape[0]
         tail = m_all[j, states : states + 16].astype(F32)
         wide = mm(jnp.concatenate(split(x), axis=0), m_all[j, 0:states], dims)
         return wide[0:count] + wide[count:] + x * (tail[0:1] + tail[1:2])
 
-    x = jnp.concatenate(
-        [jnp.zeros((rows, states), F32), jnp.where(eye, 1.0, 0.0).astype(F32)], axis=0
-    )
-    y = jnp.zeros((rows, states), F32)
+    unit = jnp.where(eye, 1.0, 0.0).astype(F32)
+    ahead = unit
+    behind = unit
     for lap in range(group):
-        late = group - 1 - lap
-        if lap == 0:
-            x_rows = u_all[0, 0].astype(F32)
-            y = u_all[late, 1].astype(F32)
-            product = advance(x[rows:], 0, NT)
-        else:
-            x = advance(jnp.concatenate([x_rows, product], axis=0), lap, NT)
-            x_rows = x[0:rows] + u_all[lap, 0].astype(F32)
-            product = x[rows:]
-            y = advance(y, late, NN) + u_all[late, 1].astype(F32)
-    tail_acc[0] = x_rows
-    tail_acc[1] = y
-    top, rest = split(product)
-    spread = (jnp.concatenate([top, rest], axis=0), jnp.concatenate([top, rest], axis=1))
+        span = slice(lap * states, (lap + 1) * states)
+        ahead = advance(ahead, lap, NT)
+        behind = advance(behind, group - 1 - lap, NN)
+        prod[0, :, span] = jnp.concatenate(split(ahead), axis=0)
+        prod[1, :, span] = jnp.concatenate(split(behind), axis=0)
+
+    firsts = (plane == 0, plane == planes - 1)
+    finals = (plane == planes - 1, plane == 0)
+    towards = (plane + 1, plane - 1)
+
+    for chunk in range(chunks):
+        for i in range(1, group):
+            u_copy(chunk, place, mate(i)).wait_recv()
+        rest = pl.ds(chunk * piece, piece)
+        x = u_all[0, 0, rest].astype(F32)
+        y = u_all[group - 1, 1, rest].astype(F32)
+        local[0, rest, 0:states] = x
+        local[1, rest, 0:states] = y
+        for lap in range(1, group):
+            late = group - 1 - lap
+            span = slice(lap * states, (lap + 1) * states)
+            x = advance(x, lap, NT) + u_all[lap, 0, rest].astype(F32)
+            y = advance(y, late, NN) + u_all[late, 1, rest].astype(F32)
+            local[0, rest, span] = x
+            local[1, rest, span] = y
+        if planes > 1:
+            for part, last in enumerate((x, y)):
+
+                @pl.when(firsts[part])
+                def _():
+                    e_src[part, rest] = last.astype(BF16)
+                    e_copy(part, chunk, towards[part]).start()
+
+    for part in range(2):
+
+        @pl.when(firsts[part])
+        def _():
+            e_all[part] = jnp.zeros((rows, states), BF16)
+
+    edge = (group - 1) * states
 
     def run(part):
-        first = (plane == 0, plane == planes - 1)[part]
-        final = (plane == planes - 1, plane == 0)[part]
-        towards = (plane + 1, plane - 1)[part]
-        dims = (NN, NT)[part]
-
-        @pl.when(first)
-        def _():
-            e_src[part] = tail_acc[part].astype(BF16)
-            e_all[part] = jnp.zeros((rows, states), BF16)
-            if planes > 1:
-                for chunk in range(chunks):
-                    e_copy(part, chunk, towards).start()
-
-        @pl.when(jnp.logical_not(first))
-        def _():
-            for chunk in range(chunks):
+        for chunk in range(chunks):
+            rest = pl.ds(chunk * piece, piece)
+
+            @pl.when(jnp.logical_not(firsts[part]))
+            def _():
                 e_copy(part, chunk, plane).wait_recv()
 
-                @pl.when(jnp.logical_not(final))
+            @pl.when(jnp.logical_not(jnp.logical_or(firsts[part], finals[part])))
+            def _():
+                entered = e_all[part, rest]
+                left = mm(jnp.concatenate([entered, entered], axis=1), prod[part, :, edge:], NN)
+                e_src[part, rest] = (left + local[part, rest, edge:]).astype(BF16)
+                e_copy(part, chunk, towards[part]).start()
+
+            entered = e_all[part, rest]
+            doubled = jnp.concatenate([entered, entered], axis=1)
+            for lap in range(group):
+                j = (lap, group - 1 - lap)[part]
+                if lap == 0:
+                    state = entered
+                else:
+                    span = slice((lap - 1) * states, lap * states)
+                    state = (mm(doubled, prod[part, :, span], NN) + local[part, rest, span]).astype(
+                        BF16
+                    )
+                s_src[part, j, rest] = state
+
+                @pl.when(place != j)
                 def _():
-                    span = pl.ds(chunk * piece, piece)
-                    entered = e_all[part, span]
-                    left = mm(jnp.concatenate([entered, entered], axis=1), spread[part], dims)
-                    e_src[part, span] = (left + tail_acc[part, span]).astype(BF16)
-                    e_copy(part, chunk, towards).start()
-
-        state = e_all[part].astype(F32)
-        for lap in range(group):
-            j = (lap, group - 1 - lap)[part]
-            s_src[part, j] = state.astype(BF16)
-
-            @pl.when(place != j)
-            def _():
-                s_copy(part, j, place).start()
-
-            @pl.when(place == j)
-            def _():
-                s_all[part, slab(place)] = s_src[part, j]
-
-            if lap < group - 1:
-                state = advance(state, j, (NT, NN)[part]) + u_all[j, part].astype(F32)
+                    s_copy(part, chunk, j, place).start()
+
+                @pl.when(place == j)
+                def _():
+                    s_all[part, bit(place, chunk)] = state
 
     def collect(part):
-        for i in range(1, group):
-            s_copy(part, place, mate(i)).wait_recv()
+        for chunk in range(chunks):
+            for i in range(1, group):
+                s_copy(part, chunk, place, mate(i)).wait_recv()
 
     share = tokens // nh
     row_share = states // nh
@@ -393,10 +414,11 @@
 
     for i in range(1, group):
         target = mate(i)
-        u_copy(target, place).wait_send()
         m_copy(target, place).wait_send()
-        s_copy(0, target, place).wait_send()
-        s_copy(1, target, place).wait_send()
+        for chunk in range(chunks):
+            u_copy(chunk, target, place).wait_send()
+            s_copy(0, chunk, target, place).wait_send()
+            s_copy(1, chunk, target, place).wait_send()
     for i in range(1, nh):
         qk_copy(partner(i), core).wait_send()
         gt_copy(partner(i), core).wait_send()
@@ -465,7 +487,8 @@
             pltpu.VMEM((group, states + 16, states), BF16),
             pltpu.VMEM((2, rows, states), BF16),
             pltpu.VMEM((2, rows, states), BF16),
-            pltpu.VMEM((2, rows, states), F32),
+            pltpu.VMEM((2, 2 * states, group * states), BF16),
+            pltpu.VMEM((2, rows, group * states), F32),
             pltpu.VMEM((2, group, rows, states), BF16),
             pltpu.VMEM((2, cols, states), BF16),
             pltpu.VMEM((tokens, cols), F32),
@@ -475,14 +498,14 @@
             pltpu.VMEM((states, states), F32),
             pltpu.VMEM((nh, row_share, states), F32),
             pltpu.SemaphoreType.DMA((5,)),
-            pltpu.SemaphoreType.DMA((group,)),
-            pltpu.SemaphoreType.DMA((group,)),
+            pltpu.SemaphoreType.DMA((chunks, group)),
+            pltpu.SemaphoreType.DMA((chunks, group)),
             pltpu.SemaphoreType.DMA((group,)),
             pltpu.SemaphoreType.DMA((group,)),
             pltpu.SemaphoreType.DMA((2, chunks)),
             pltpu.SemaphoreType.DMA((2, chunks)),
-            pltpu.SemaphoreType.DMA((2, group)),
-            pltpu.SemaphoreType.DMA((2, group)),
+            pltpu.SemaphoreType.DMA((2, chunks, group)),
+            pltpu.SemaphoreType.DMA((2, chunks, group)),
             pltpu.SemaphoreType.DMA((2, nh)),
             pltpu.SemaphoreType.DMA((2, nh)),
         ],

time: 34.1 us -> 32.8 us (0.962)
  Pallas kernels: 33.3 us -> 32 us
    pallas_call x1, Pallas kernels: 32.3 us -> 31 us  [per_device(): pl.pallas_call(functools.partial(kernel, n, nh, group, chunks), out_shape...]
where the time goes in v3:
time: 32.8 us; the launch traced here: 32.7 us
  Pallas kernels  32 us (98%)
  between operations  0.64 us (2%)
    pallas_call x1, Pallas kernels, per_device(): pl.pallas_call(functools.partial(kernel, n, nh, group, chunks), out_shape...  31 us
    pallas_call x1, Pallas kernels, per_device(): pl.pallas_call(store, out_shape=shapes, in_specs=[vmem] * 5, out_specs=(a...  1.04 us

profile of v3, /device:TPU:0, one launch (start us, length us, event | category | flops | bytes accessed | tf_op | source)
XLA Modules:
  0.0 32.7 jit_solution(2824641463275352162)
XLA Ops:
  0.6 31.0 %shard_map.92 = (bf16[256,1024]{1,0:T(8,128)(2,1)S(1)}, bf16[128,128]{1,0:T(8,128)(2,1)S(1)}, bf16[128,128]{1,0:T(8,128)(2,1)S(1)}, bf16[256,1024]{1,0:T(8,128)(2,1)S(1)}, f32[64,128]{1,0:T(8,128)S(1)}) custom-call(bf16[256,128]{1,0:T(8,128)(2,1)} %q_hbm.1, bf16[256,128]{1,0:T(8,128)(2,1)} %k_hbm.1, bf16[256,1024]{1,0:T(8,128)(2,1)} %v_hbm.1, ...), custom_call_target="tpu_custom_call" | custom-call | tf_op jit(solution)/shard_map/pallas_call | solution.py:473
  31.6 1.0 %shard_map.93 = (bf16[256,1024]{1,0:T(8,128)(2,1)}, bf16[128,128]{1,0:T(8,128)(2,1)}, bf16[128,128]{1,0:T(8,128)(2,1)}, bf16[256,1024]{1,0:T(8,128)(2,1)}, f32[64,128]{1,0:T(8,128)}) custom-call(bf16[256,1024]{1,0:T(8,128)(2,1)S(1)} %get-tuple-element.15.refs_0_, bf16[128,128]{1,0:T(8,128)(2,1)S(1)} %get-tuple-element.16.refs_1_, ...), custom_call_target="tpu_custom_call" | custom-call | tf_op jit(solution)/shard_map/pallas_call | solution.py:516

commit v4 on v3

--- a/solution.py
+++ b/solution.py
@@ -64,6 +64,8 @@
     u_all,
     m_src,
     m_all,
+    a_src,
+    a_all,
     e_src,
     e_all,
     prod,
@@ -81,6 +83,8 @@
     u_recv,
     m_send,
     m_recv,
+    a_send,
+    a_recv,
     e_send,
     e_recv,
     s_send,
@@ -141,13 +145,8 @@
     for i in range(1, nh):
         signal({"seq": me, "head": partner(i)})
 
-    @pl.when(plane > 0)
-    def _():
-        signal(at_plane(plane - 1))
-
-    @pl.when(plane < planes - 1)
-    def _():
-        signal(at_plane(plane + 1))
+    for i in range(1, planes):
+        signal(at_plane(lax.rem(plane + i, planes)))
 
     for copy in loads:
         copy.wait()
@@ -160,17 +159,19 @@
     eye = lax.broadcasted_iota(jnp.int32, (states, states), 0) == lax.broadcasted_iota(
         jnp.int32, (states, states), 1
     )
-    diagonal = jnp.sum(jnp.where(eye, transition, 0.0), axis=0, keepdims=True)
-    high = diagonal.astype(BF16).astype(F32)
     line = lax.broadcasted_iota(jnp.int32, (16, states), 0)
-    m_src[0:states] = jnp.where(eye, 0.0, transition).astype(BF16)
-    m_src[states : states + 16] = jnp.where(
-        line == 0, high, jnp.where(line == 1, diagonal - high, 0.0)
-    ).astype(BF16)
-
-    above = lax.min(plane, 1)
-    below = lax.min(planes - 1 - plane, 1)
-    pl.semaphore_wait(barrier, group - 1 + nh - 1 + above + below)
+
+    def encode(ref, full):
+        diagonal = jnp.sum(jnp.where(eye, full, 0.0), axis=0, keepdims=True)
+        high = diagonal.astype(BF16).astype(F32)
+        ref[0:states] = jnp.where(eye, 0.0, full).astype(BF16)
+        ref[states : states + 16] = jnp.where(
+            line == 0, high, jnp.where(line == 1, diagonal - high, 0.0)
+        ).astype(BF16)
+
+    encode(m_src, transition)
+
+    pl.semaphore_wait(barrier, group - 1 + nh - 1 + planes - 1)
 
     def slab(j):
         return pl.ds(pl.multiple_of(j * rows, rows), rows)
@@ -198,13 +199,23 @@
             device_id_type=MESH,
         )
 
-    def e_copy(part, chunk, target):
+    def a_copy(target, source):
+        return pltpu.make_async_remote_copy(
+            src_ref=a_src,
+            dst_ref=a_all.at[source],
+            send_sem=a_send.at[target],
+            recv_sem=a_recv.at[source],
+            device_id=at_plane(target),
+            device_id_type=MESH,
+        )
+
+    def e_copy(part, chunk, target, source):
         span = pl.ds(chunk * piece, piece)
         return pltpu.make_async_remote_copy(
             src_ref=e_src.at[part, span],
-            dst_ref=e_all.at[part, span],
-            send_sem=e_send.at[part, chunk],
-            recv_sem=e_recv.at[part, chunk],
+            dst_ref=e_all.at[part, source, span],
+            send_sem=e_send.at[part, chunk, target],
+            recv_sem=e_recv.at[part, chunk, source],
             device_id=at_plane(target),
             device_id_type=MESH,
         )
@@ -246,11 +257,14 @@
 
     for i in range(1, group):
         m_copy(place, mate(i)).wait_recv()
+    def apply(x, ref, j, dims):
+        count = x.shape[0]
+        tail = ref[j, states : states + 16].astype(F32)
+        wide = mm(jnp.concatenate(split(x), axis=0), ref[j, 0:states], dims)
+        return wide[0:count] + wide[count:] + x * (tail[0:1] + tail[1:2])
+
     def advance(x, j, dims):
-        count = x.shape[0]
-        tail = m_all[j, states : states + 16].astype(F32)
-        wide = mm(jnp.concatenate(split(x), axis=0), m_all[j, 0:states], dims)
-        return wide[0:count] + wide[count:] + x * (tail[0:1] + tail[1:2])
+        return apply(x, m_all, j, dims)
 
     unit = jnp.where(eye, 1.0, 0.0).astype(F32)
     ahead = unit
@@ -262,9 +276,9 @@
         prod[0, :, span] = jnp.concatenate(split(ahead), axis=0)
         prod[1, :, span] = jnp.concatenate(split(behind), axis=0)
 
-    firsts = (plane == 0, plane == planes - 1)
-    finals = (plane == planes - 1, plane == 0)
-    towards = (plane + 1, plane - 1)
+    encode(a_src, behind)
+    for i in range(1, planes):
+        a_copy(lax.rem(plane + i, planes), plane).start()
 
     for chunk in range(chunks):
         for i in range(1, group):
@@ -281,38 +295,37 @@
             y = advance(y, late, NN) + u_all[late, 1, rest].astype(F32)
             local[0, rest, span] = x
             local[1, rest, span] = y
-        if planes > 1:
-            for part, last in enumerate((x, y)):
-
-                @pl.when(firsts[part])
-                def _():
-                    e_src[part, rest] = last.astype(BF16)
-                    e_copy(part, chunk, towards[part]).start()
-
-    for part in range(2):
-
-        @pl.when(firsts[part])
-        def _():
-            e_all[part] = jnp.zeros((rows, states), BF16)
-
-    edge = (group - 1) * states
+        e_src[0, rest] = x.astype(BF16)
+        e_src[1, rest] = y.astype(BF16)
+        for i in range(1, planes):
+
+            @pl.when(plane + i < planes)
+            def _():
+                e_copy(0, chunk, plane + i, plane).start()
+
+            @pl.when(plane - i >= 0)
+            def _():
+                e_copy(1, chunk, plane - i, plane).start()
+
+    for i in range(1, planes):
+        a_copy(plane, lax.rem(plane + i, planes)).wait_recv()
 
     def run(part):
         for chunk in range(chunks):
             rest = pl.ds(chunk * piece, piece)
 
-            @pl.when(jnp.logical_not(firsts[part]))
-            def _():
-                e_copy(part, chunk, plane).wait_recv()
-
-            @pl.when(jnp.logical_not(jnp.logical_or(firsts[part], finals[part])))
-            def _():
-                entered = e_all[part, rest]
-                left = mm(jnp.concatenate([entered, entered], axis=1), prod[part, :, edge:], NN)
-                e_src[part, rest] = (left + local[part, rest, edge:]).astype(BF16)
-                e_copy(part, chunk, towards[part]).start()
-
-            entered = e_all[part, rest]
+            def hop(i, held):
+                source = (i, planes - 1 - i)[part]
+                e_copy(part, chunk, plane, source).wait_recv()
+                moved = apply(held, a_all, source, (NT, NN)[part])
+                return moved + e_all[part, source, rest].astype(F32)
+
+            entered = lax.fori_loop(
+                0,
+                (plane, planes - 1 - plane)[part],
+                hop,
+                jnp.zeros((piece, states), F32),
+            ).astype(BF16)
             doubled = jnp.concatenate([entered, entered], axis=1)
             for lap in range(group):
                 j = (lap, group - 1 - lap)[part]
@@ -423,15 +436,18 @@
         qk_copy(partner(i), core).wait_send()
         gt_copy(partner(i), core).wait_send()
 
-    @pl.when(plane < planes - 1)
-    def _():
-        for chunk in range(chunks):
-            e_copy(0, chunk, plane + 1).wait_send()
-
-    @pl.when(plane > 0)
-    def _():
-        for chunk in range(chunks):
-            e_copy(1, chunk, plane - 1).wait_send()
+    for i in range(1, planes):
+        a_copy(lax.rem(plane + i, planes), plane).wait_send()
+
+        @pl.when(plane + i < planes)
+        def _():
+            for chunk in range(chunks):
+                e_copy(0, chunk, plane + i, plane).wait_send()
+
+        @pl.when(plane - i >= 0)
+        def _():
+            for chunk in range(chunks):
+                e_copy(1, chunk, plane - i, plane).wait_send()
 
 
 def store(*refs):
@@ -485,8 +501,10 @@
             pltpu.VMEM((group, 2, rows, states), BF16),
             pltpu.VMEM((states + 16, states), BF16),
             pltpu.VMEM((group, states + 16, states), BF16),
+            pltpu.VMEM((states + 16, states), BF16),
+            pltpu.VMEM((n // group, states + 16, states), BF16),
             pltpu.VMEM((2, rows, states), BF16),
-            pltpu.VMEM((2, rows, states), BF16),
+            pltpu.VMEM((2, n // group, rows, states), BF16),
             pltpu.VMEM((2, 2 * states, group * states), BF16),
             pltpu.VMEM((2, rows, group * states), F32),
             pltpu.VMEM((2, group, rows, states), BF16),
@@ -502,8 +520,10 @@
             pltpu.SemaphoreType.DMA((chunks, group)),
             pltpu.SemaphoreType.DMA((group,)),
             pltpu.SemaphoreType.DMA((group,)),
-            pltpu.SemaphoreType.DMA((2, chunks)),
-            pltpu.SemaphoreType.DMA((2, chunks)),
+            pltpu.SemaphoreType.DMA((n // group,)),
+            pltpu.SemaphoreType.DMA((n // group,)),
+            pltpu.SemaphoreType.DMA((2, chunks, n // group)),
+            pltpu.SemaphoreType.DMA((2, chunks, n // group)),
             pltpu.SemaphoreType.DMA((2, chunks, group)),
             pltpu.SemaphoreType.DMA((2, chunks, group)),
             pltpu.SemaphoreType.DMA((2, nh)),

time: 32.8 us -> 29.5 us (0.90)
  Pallas kernels: 32 us -> 28.7 us
    pallas_call x1, Pallas kernels: 31 us -> 27.7 us  [per_device(): pl.pallas_call(functools.partial(kernel, n, nh, group, chunks), out_shape...]
where the time goes in v4:
time: 29.5 us; the launch traced here: 29.3 us
  Pallas kernels  28.7 us (97%)
  between operations  0.64 us (2%)
    pallas_call x1, Pallas kernels, per_device(): pl.pallas_call(functools.partial(kernel, n, nh, group, chunks), out_shape...  27.7 us
    pallas_call x1, Pallas kernels, per_device(): pl.pallas_call(store, out_shape=shapes, in_specs=[vmem] * 5, out_specs=(a...  1.04 us

profile of v4, /device:TPU:0, one launch (start us, length us, event | category | flops | bytes accessed | tf_op | source)
XLA Modules:
  0.0 29.3 jit_solution(15774992073239340960)
XLA Ops:
  0.6 27.7 %shard_map.92 = (bf16[256,1024]{1,0:T(8,128)(2,1)S(1)}, bf16[128,128]{1,0:T(8,128)(2,1)S(1)}, bf16[128,128]{1,0:T(8,128)(2,1)S(1)}, bf16[256,1024]{1,0:T(8,128)(2,1)S(1)}, f32[64,128]{1,0:T(8,128)S(1)}) custom-call(bf16[256,128]{1,0:T(8,128)(2,1)} %q_hbm.1, bf16[256,128]{1,0:T(8,128)(2,1)} %k_hbm.1, bf16[256,1024]{1,0:T(8,128)(2,1)} %v_hbm.1, ...), custom_call_target="tpu_custom_call" | custom-call | tf_op jit(solution)/shard_map/pallas_call | solution.py:489
  28.3 1.0 %shard_map.93 = (bf16[256,1024]{1,0:T(8,128)(2,1)}, bf16[128,128]{1,0:T(8,128)(2,1)}, bf16[128,128]{1,0:T(8,128)(2,1)}, bf16[256,1024]{1,0:T(8,128)(2,1)}, f32[64,128]{1,0:T(8,128)}) custom-call(bf16[256,1024]{1,0:T(8,128)(2,1)S(1)} %get-tuple-element.15.refs_0_, bf16[128,128]{1,0:T(8,128)(2,1)S(1)} %get-tuple-element.16.refs_1_, ...), custom_call_target="tpu_custom_call" | custom-call | tf_op jit(solution)/shard_map/pallas_call | solution.py:536
